TPU v7x, 256 devices: a whole 4x4x8 slice. The times are simulated.
256 devices in a mesh: band: 4 (over x_lo, core), fft: 64 (over z, x_hi, y).
Axes of the slice: x: 4 (x_hi: 2, x_lo: 2; x = x_hi * 2 + x_lo), y: 4, z: 8, core: 2. Of those that a mesh axis runs over, the one named last changes fastest.
Arguments:
- orbitals: float32 [4, 128, 128, 128], P('band', 'fft'), may hold values from -6 to 6
- stick_cols: int32 [8192], replicated, may hold values from 0 to 16383, as said below
Outputs:
- exchange_field: float32 [4, 128, 128, 128], P('band', 'fft')
- spectrum: float32 [4, 128, 8192], P('band', None, 'fft')
Inputs may be any that keep to these rules, and one draw needn't show every extreme that they name: `stick_cols`: distinct flat column indices kx * 128 + ky; every column with s(kx)^2 + s(ky)^2 <= 48^2 is listed, the other entries are further columns, all in a drawn order.
All inputs are finite; a program needn't handle non-finite values.
Results may differ from a plain program's by a relative error of at most 0.0003.
Values sent between devices are 32-bit elements; how exact they have to be, the bound alone decides.
A program may use at most 64 MiB of HBM per device.

v0:
```python
import math

import jax
import jax.numpy as jnp
import numpy as np
from jax import lax
from jax.sharding import PartitionSpec as P

RAD = 48


screening = 16.0
strength = 10.0
highest = lax.Precision.HIGHEST


def from_behind(block, axis, distance):
    devices = range(lax.axis_size(axis))
    route = [((i - distance) % len(devices), i) for i in devices]
    return lax.ppermute(block, axis, route)


def cas_table(grid_len):
    positions = jnp.arange(grid_len, dtype=jnp.int32)
    phases = positions[:, None] * positions[None, :] % grid_len
    angles = 2.0 * math.pi / grid_len * phases.astype(jnp.float32)
    return (jnp.cos(angles) + jnp.sin(angles)) / math.sqrt(grid_len)


def signed(positions, grid_len):
    return jnp.where(positions < grid_len // 2, positions, positions - grid_len)


def coulomb(squared):
    kappa_float = squared.astype(jnp.float32)
    safe_kappa = jnp.maximum(kappa_float, jnp.float32(1.0))
    values = strength * screening * (1.0 - jnp.exp(-kappa_float / screening)) / safe_kappa
    inside = (squared > 0) & (squared <= RAD * RAD)
    return jnp.where(inside, values, jnp.float32(0.0))


def body(orbitals, stick_cols):
    local_bands, planes, grid_len, _ = orbitals.shape
    sticks_dev = stick_cols.shape[0] // lax.axis_size("fft")
    cas_rows = cas_table(grid_len)
    offset_start = lax.axis_index("fft") * sticks_dev
    own_sticks = lax.dynamic_slice_in_dim(stick_cols, offset_start, sticks_dev)
    row_signed = signed(own_sticks // grid_len, grid_len)
    col_signed = signed(own_sticks % grid_len, grid_len)
    along_z = signed(jnp.arange(grid_len, dtype=jnp.int32), grid_len)
    kernel = coulomb(
        (along_z * along_z)[:, None] + (row_signed * row_signed + col_signed * col_signed)[None, :]
    )
    band_ids = np.arange(local_bands)
    previous = from_behind(orbitals, "band", 1)
    every_first = np.repeat(band_ids, local_bands)
    every_second = np.tile(band_ids, local_bands)
    no_mirror = np.zeros(local_bands * local_bands, dtype=bool)
    own_pairs = (every_first, every_second, no_mirror)
    prev_pairs = (every_first, every_second, no_mirror)
    totals = (
        jnp.zeros(orbitals.shape, jnp.float32),
        jnp.zeros((local_bands, grid_len, sticks_dev), jnp.float32),
    )
    for partner, pair_lists in ((orbitals, own_pairs), (previous, prev_pairs)):
        first_ids, second_ids, mirror = pair_lists
        chosen = first_ids == 0
        if chosen.any():
            accumulate_first_ids = first_ids[chosen]
            accumulate_second_ids = second_ids[chosen]
            accumulate_mirror = mirror[chosen]
            accumulate_field_sum, accumulate_spectrum_sum = totals
            source = orbitals[accumulate_first_ids]
            pair_partner = partner[accumulate_second_ids]
            pair_count = source.shape[0]
            density = source * pair_partner
            half_done = jnp.einsum("pzxy,yk->pzxk", density, cas_rows, precision=highest)
            plane_done = jnp.einsum("pzxk,xj->pzjk", half_done, cas_rows, precision=highest)
            flat_planes = plane_done.reshape(pair_count, planes, grid_len * grid_len)
            columns = jnp.take(flat_planes, stick_cols, axis=2)
            spectral = jnp.einsum(
                "pzs,zk->pks",
                lax.all_to_all(columns, "fft", split_axis=2, concat_axis=1, tiled=True),
                cas_rows,
                precision=highest,
            )
            weighted = kernel[None] * spectral
            energy = weighted * spectral
            potential = jnp.einsum("pks,kz->pzs", weighted, cas_rows, precision=highest)
            returned = lax.all_to_all(potential, "fft", split_axis=1, concat_axis=2, tiled=True)
            filled = jnp.zeros((pair_count, planes, grid_len * grid_len), jnp.float32)
            filled = filled.at[:, :, stick_cols].set(returned)
            filled = filled.reshape(pair_count, planes, grid_len, grid_len)
            half_back = jnp.einsum("pzjk,jx->pzxk", filled, cas_rows, precision=highest)
            pair_potential = jnp.einsum("pzxk,ky->pzxy", half_back, cas_rows, precision=highest)
            credit = (band_ids[:, None] == accumulate_first_ids[None, :]).astype(np.float32)
            reverse = (
                (band_ids[:, None] == accumulate_second_ids[None, :]) & accumulate_mirror[None, :]
            ).astype(np.float32)
            accumulate_field_sum = accumulate_field_sum - jnp.einsum(
                "bp,pzxy->bzxy",
                credit,
                pair_potential * partner[accumulate_second_ids],
                precision=highest,
            )
            if accumulate_mirror.any():
                accumulate_field_sum = accumulate_field_sum - jnp.einsum(
                    "bp,pzxy->bzxy",
                    reverse,
                    pair_potential * orbitals[accumulate_first_ids],
                    precision=highest,
                )
            accumulate_spectrum_sum = accumulate_spectrum_sum + jnp.einsum(
                "bp,pks->bks", credit + reverse, energy, precision=highest
            )
            totals = (accumulate_field_sum, accumulate_spectrum_sum)
    field_sum, spectrum_sum = totals
    return (field_sum, spectrum_sum / jnp.float32(2 * local_bands))


def solution(mesh):
    return jax.shard_map(
        body,
        mesh=mesh,
        in_specs=(P("band", "fft", None, None), P()),
        out_specs=(P("band", "fft", None, None), P("band", None, "fft")),
        check_vma=False,
    )
```

profile of v0, /device:TPU:58, one launch (start us, length us, event | category | flops | bytes accessed | tf_op | source)
XLA Modules:
  0.0 323.9 jit_solution(9609663205031424347)
XLA Ops:
  0.7 1.4 fusion.9
  2.2 0.8 broadcast_clamp_fusion
  3.5 4.6 %copy.62 = f32[1,2,128,128]{1,3,2,0:T(8,128)} copy(f32[1,2,128,128]{3,2,1,0:T(8,128)S(1)} %convolution_bitcast_fusion.3) | data formatting | bytes 262144 | tf_op jit(solution)/shard_map/reshape | solution.py:79
  8.2 31.1 %gather_fusion = f32[8192,2]{1,0:T(8,128)} fusion(f32[2,16384]{0,1:T(8,128)} %bitcast.126, s32[8192]{0:T(1024)S(1)} %get-tuple-element.3), kind=kCustom, calls=%fused_computation.clone | custom fusion | bytes 163840 | tf_op jit(solution)/shard_map/jit(_take)/gather | solution.py:80
  40.4 4.6 %copy.65 = f32[1,2,128,128]{1,3,2,0:T(8,128)} copy(f32[1,2,128,128]{3,2,1,0:T(8,128)S(1)} %convolution_bitcast_fusion.1) | data formatting | bytes 262144 | tf_op jit(solution)/shard_map/reshape | solution.py:79
  45.1 31.1 %gather_fusion.1 = f32[8192,2]{1,0:T(8,128)} fusion(f32[2,16384]{0,1:T(8,128)} %bitcast.125, s32[8192]{0:T(1024)S(1)} %get-tuple-element.3), kind=kCustom, calls=%fused_computation.1.clone | custom fusion | bytes 163840 | tf_op jit(solution)/shard_map/jit(_take)/gather | solution.py:80
  76.1 7.3 %bitcast_select_fusion.1 = (f32[1,2,8192]{1,2,0:T(8,128)}, f32[1,2,8192]{1,2,0:T(8,128)}) fusion(f32[8192,2]{1,0:T(8,128)} %gather_fusion, pred[8192]{0:T(1024)(128)(4,1)S(1)} %compare_and_fusion, f32[8192,2]{1,0:T(8,128)} %gather_fusion.1), kind=kLoop, calls=%fused_computation.5 | loop fusion | flops 32768 | bytes 270336 | tf_op jit(solution)/shard_map/jit(_take)/select_n | solution.py:80
  84.0 38.3 %reduce.2 = f32[8192,2]{1,0:T(8,128)} reduce(f32[8192,1,2]{2,1,0:T(1,128)} %bitcast.124, f32[]{:T(128)} %broadcast.176), dimensions={1}, to_apply=%bitcast.107.reduce_sub_computation | reduce | bytes 131076
  122.2 5.1 %reshape.239 = f32[64,1,256]{2,1,0:T(1,128)} reshape(f32[8192,2]{1,0:T(8,128)} %reduce.2) | data formatting | bytes 131072
  127.4 13.0 %all-to-all-start = ((f32[64,1,256]{2,1,0:T(1,128)}), f32[64,1,256]{2,1,0:T(1,128)S(1)}, u32[]{:S(2)}, u32[]{:S(2)}) async-start(f32[64,1,256]{2,1,0:T(1,128)} %reshape.239), calls=%async_computation | async-start | bytes 131072 | tf_op jit(solution)/shard_map/all_to_all | solution.py:83
  140.5 38.3 %reduce = f32[8192,2]{1,0:T(8,128)} reduce(f32[8192,1,2]{2,1,0:T(1,128)} %bitcast.123, f32[]{:T(128)} %broadcast.176), dimensions={1}, to_apply=%bitcast.105.reduce_sub_computation | reduce | bytes 131076
  178.7 5.1 %reshape.237 = f32[64,1,256]{2,1,0:T(1,128)} reshape(f32[8192,2]{1,0:T(8,128)} %reduce) | data formatting | bytes 131072
  183.9 12.7 %all-to-all-start.2 = ((f32[64,1,256]{2,1,0:T(1,128)}), f32[64,1,256]{2,1,0:T(1,128)S(1)}, u32[]{:S(2)}, u32[]{:S(2)}) async-start(f32[64,1,256]{2,1,0:T(1,128)} %reshape.237), calls=%async_computation.2 | async-start | bytes 131072 | tf_op jit(solution)/shard_map/all_to_all | solution.py:83
  196.6 0.7 reduce.3
  197.3 8.1 %reshape.240 = f32[8192,1,2]{2,1,0:T(1,128)} reshape(f32[64,256]{1,0:T(8,128)S(1)} %reduce.3) | data formatting | bytes 131072
  205.4 2.8 copy.43
  208.8 1.2 fusion.40
  210.0 12.7 %all-to-all-start.1 = ((f32[1,128,128]{2,0,1:T(1,128)}), f32[1,128,128]{2,0,1:T(1,128)S(1)}, u32[]{:S(2)}, u32[]{:S(2)}) async-start(f32[1,128,128]{2,0,1:T(1,128)} %bitcast.15), calls=%async_computation.1 | async-start | bytes 131072 | tf_op jit(solution)/shard_map/all_to_all | solution.py:90
  222.7 0.7 reduce.1
  223.5 8.1 %reshape.238 = f32[8192,1,2]{2,1,0:T(1,128)} reshape(f32[64,256]{1,0:T(8,128)S(1)} %reduce.1) | data formatting | bytes 131072
  231.5 2.8 copy.51
  234.9 1.2 fusion.38
  236.2 12.7 %all-to-all-start.3 = ((f32[1,128,128]{2,0,1:T(1,128)}), f32[1,128,128]{2,0,1:T(1,128)S(1)}, u32[]{:S(2)}, u32[]{:S(2)}) async-start(f32[1,128,128]{2,0,1:T(1,128)} %bitcast.39), calls=%async_computation.3 | async-start | bytes 131072 | tf_op jit(solution)/shard_map/all_to_all | solution.py:90
  248.9 0.7 fusion.33
  249.6 2.6 copy.45
  252.2 6.6 %all-to-all-done.3 = f32[1,128,128]{2,0,1:T(1,128)S(1)} async-done(((f32[1,128,128]{2,0,1:T(1,128)}), f32[1,128,128]{2,0,1:T(1,128)S(1)}, u32[]{:S(2)}, u32[]{:S(2)}) %all-to-all-start.3) | async-done | bytes 65568 | tf_op jit(solution)/shard_map/all_to_all | solution.py:90
  258.8 2.6 copy.53
  261.5 24.5 %scatter_custom_fusion.1 = f32[2,16384]{0,1:T(8,128)} fusion(s32[8192]{0:T(1024)S(1)} %get-tuple-element.4, f32[8192,2]{1,0:T(8,128)} %bitcast.128, f32[]{:T(128)} %constant.43.clone.1), kind=kCustom, calls=%fused_computation.6 | custom fusion | bytes 131584 | tf_op jit(solution)/shard_map/scatter | solution.py:92
  286.0 5.2 %copy.55 = f32[2,128,128]{2,1,0:T(8,128)S(1)} copy(f32[2,128,128]{0,2,1:T(8,128)} %bitcast.120) | data formatting | bytes 262144 | tf_op jit(solution)/shard_map/reshape.34
  292.3 24.5 %scatter_custom_fusion = f32[2,16384]{0,1:T(8,128)} fusion(s32[8192]{0:T(1024)S(1)} %get-tuple-element.4, f32[8192,2]{1,0:T(8,128)} %bitcast.127, f32[]{:T(128)} %constant.43.clone.1), kind=kCustom, calls=%fused_computation.8 | custom fusion | bytes 131584 | tf_op jit(solution)/shard_map/scatter | solution.py:92
  316.9 5.2 %copy.47 = f32[2,128,128]{2,1,0:T(8,128)S(1)} copy(f32[2,128,128]{0,2,1:T(8,128)} %bitcast.119) | data formatting | bytes 262144 | tf_op jit(solution)/shard_map/reshape.17
  322.7 1.2 fusion.6
  (20 shorter events, 5.2 us)
Async XLA Ops:
  0.6 38.7 %collective-permute-start = (f32[1,2,128,128]{3,2,1,0:T(8,128)}, f32[1,2,128,128]{3,2,1,0:T(8,128)S(1)}, u32[]{:S(2)}, u32[]{:S(2)}) collective-permute-start(f32[1,2,128,128]{3,2,1,0:T(8,128)} %param.18), channel_id=1, source_target_pairs={{192,0},{0,64},{64,128},{128,192},{193,1},{1,65},{65,129},{129,193... | collective-permute-start | bytes 393224 | tf_op jit(solution)/shard_map/ppermute | solution.py:20
  3.5 35.8 %copy-start.1 = (s32[8192]{0:T(1024)S(1)}, s32[8192]{0:T(1024)}, u32[]{:S(2)}) copy-start(s32[8192]{0:T(1024)} %param.19) | copy-start | bytes 98308
  3.5 35.8 %copy-start = (f32[1,2,128,128]{3,2,1,0:T(8,128)S(1)}, f32[1,2,128,128]{3,2,1,0:T(8,128)}, u32[]{:S(2)}) copy-start(f32[1,2,128,128]{3,2,1,0:T(8,128)} %param.18) | copy-start | bytes 393220
  127.4 56.5 %all-to-all-start = ((f32[64,1,256]{2,1,0:T(1,128)}), f32[64,1,256]{2,1,0:T(1,128)S(1)}, u32[]{:S(2)}, u32[]{:S(2)}) async-start(f32[64,1,256]{2,1,0:T(1,128)} %reshape.239), calls=%async_computation | async-start | bytes 131072 | tf_op jit(solution)/shard_map/all_to_all | solution.py:83
  183.9 26.1 %all-to-all-start.2 = ((f32[64,1,256]{2,1,0:T(1,128)}), f32[64,1,256]{2,1,0:T(1,128)S(1)}, u32[]{:S(2)}, u32[]{:S(2)}) async-start(f32[64,1,256]{2,1,0:T(1,128)} %reshape.237), calls=%async_computation.2 | async-start | bytes 131072 | tf_op jit(solution)/shard_map/all_to_all | solution.py:83
  210.0 26.1 %all-to-all-start.1 = ((f32[1,128,128]{2,0,1:T(1,128)}), f32[1,128,128]{2,0,1:T(1,128)S(1)}, u32[]{:S(2)}, u32[]{:S(2)}) async-start(f32[1,128,128]{2,0,1:T(1,128)} %bitcast.15), calls=%async_computation.1 | async-start | bytes 131072 | tf_op jit(solution)/shard_map/all_to_all | solution.py:90
  236.2 22.7 %all-to-all-start.3 = ((f32[1,128,128]{2,0,1:T(1,128)}), f32[1,128,128]{2,0,1:T(1,128)S(1)}, u32[]{:S(2)}, u32[]{:S(2)}) async-start(f32[1,128,128]{2,0,1:T(1,128)} %bitcast.39), calls=%async_computation.3 | async-start | bytes 131072 | tf_op jit(solution)/shard_map/all_to_all | solution.py:90
where the time goes:
time: 327 us; the launch traced here: 324 us
  local copies, waits for them, and re-layouts  169 us (52%)
  other arithmetic  86.9 us (27%)
  starting transfers between devices  51.2 us (16%)
  matrix products  9.52 us (3%)
  waiting for transfers between devices  6.61 us (2%)
    unnamed x2, other arithmetic  76.6 us
    gather x2, local copies, waits for them, and re-layouts, body(): columns = jnp.take(flat_planes, stick_cols, axis=2)  62.2 us
    scatter x2, local copies, waits for them, and re-layouts, body(): filled = filled.at[:, :, stick_cols].set(returned)  49.1 us
    unnamed x9, local copies, waits for them, and re-layouts  26.9 us
    all_to_all x2, starting transfers between devices, body(): lax.all_to_all(columns, 'fft', split_axis=2, concat_axis=1, tiled=True)  25.7 us
    all_to_all x2, starting transfers between devices, body(): lax.all_to_all(potential, 'fft', split_axis=1, concat_axis=2, tiled=True)  25.4 us
    another operation x2, local copies, waits for them, and re-layouts  10.4 us
    reshape x2, local copies, waits for them, and re-layouts, body(): flat_planes = plane_done.reshape(pair_count, planes, grid_len * grid_len)  9.28 us
  transfers between devices with their start and end apart: 5, of which 1 were waited for; matrix products, arithmetic and copies ran while one was open for 35% of the time, Pallas kernels for 0%

commit v1 on v0

v1 whole, which is shorter than its diff:
```python
import functools
import math

import jax
import jax.numpy as jnp
import numpy as np
from jax import lax
from jax.experimental import pallas as pl
from jax.experimental.pallas import tpu as pltpu
from jax.sharding import PartitionSpec as P

RAD = 48
N = 128
NF = 64
NBAND = 4
NOWN = 32
PER = 4
STEPS = NOWN // PER
LANES = PER * 2 * N

screening = 16.0
strength = 10.0

MESH = pl.DeviceIdType.MESH
f32 = jnp.float32
bf16 = jnp.bfloat16


def owner_device(o):
    return o


def partner_block(o):
    return o + NOWN


def tables():
    k = np.arange(N)
    angles = 2.0 * math.pi / N * (k[:, None] * k[None, :] % N)
    c = (np.cos(angles) + np.sin(angles)) / math.sqrt(N)
    import ml_dtypes

    hi = c.astype(np.float32).astype(ml_dtypes.bfloat16)
    lo = (c - hi.astype(np.float64)).astype(np.float32).astype(ml_dtypes.bfloat16)
    order = np.concatenate([k[0::2], k[1::2]])
    along_y = np.block([[hi, lo], [hi, lo]])
    split_rows = np.block([[hi[order], hi[order]], [lo[order], lo[order]]])
    split_cols = np.block([[hi[:, order], hi[:, order]], [lo[:, order], lo[:, order]]])
    return along_y, split_rows, split_cols


def two_terms(x):
    hi = x.astype(bf16)
    return hi, (x - hi.astype(f32)).astype(bf16)


def signed(x):
    return jnp.where(x < N // 2, x, x - N)


def coulomb(squared):
    kappa = squared.astype(f32)
    safe = jnp.maximum(kappa, f32(1.0))
    values = strength * screening * (1.0 - jnp.exp(-kappa / screening)) / safe
    inside = (squared > 0) & (squared <= RAD * RAD)
    return jnp.where(inside, values, f32(0.0))


def dot(a, b):
    return jnp.dot(a, b, preferred_element_type=f32)


def left_table(table, x):
    hi, lo = two_terms(x)
    both = dot(table, jnp.concatenate([hi, lo], axis=0))
    return both[:N] + both[N:]


def right_table(x, table):
    hi, lo = two_terms(x)
    both = dot(jnp.concatenate([hi, lo], axis=1), table)
    return both[:, :N] + both[:, N:]


def kernel(
    orb_hbm, cols, taby_hbm, tabf_hbm, tabi_hbm, field, spec,
    own, prev, taby, tabf, tabi, pick, rowf, rowb, send1, recv1, send2, recv2, wide, acc, en,
    load_sem, orb_sem, out1_sem, in1_sem, out2_sem, in2_sem, en_sem,
):
    me = lax.axis_index("fft")
    band = lax.axis_index("band")
    is_owner = me < NOWN
    before = lax.rem(band + NBAND - 1, NBAND)
    after = lax.rem(band + 1, NBAND)

    loads = [
        pltpu.make_async_copy(src, dst, load_sem.at[i])
        for i, (src, dst) in enumerate(
            ((orb_hbm, own), (taby_hbm, taby), (tabf_hbm, tabf), (tabi_hbm, tabi))
        )
    ]
    for load in loads:
        load.start()

    barrier = pltpu.get_barrier_semaphore()
    pl.semaphore_signal(barrier, inc=1, device_id={"band": before}, device_id_type=MESH)

    @pl.when(is_owner)
    def _():
        def greet(i, carry):
            pl.semaphore_signal(
                barrier, inc=1, device_id={"fft": lax.rem(me + i, NF)}, device_id_type=MESH
            )
            return carry

        lax.fori_loop(1, NF, greet, 0)

    low_iota = lax.broadcasted_iota(jnp.int32, (2 * N, N), 0)
    high_iota = lax.broadcasted_iota(jnp.int32, (N // 2, N), 0)

    def build(o, carry):
        for blk, source in enumerate((owner_device(o), partner_block(o))):
            flat = cols[pl.ds(source, 1), :]
            lanes = pl.ds(pl.multiple_of((2 * o + blk) * N, N), N)
            pick[:, lanes] = jnp.where(low_iota == lax.rem(flat, 2 * N), 1.0, 0.0).astype(bf16)
            high = jnp.where(high_iota == lax.div(flat, 2 * N), f32(1.0), f32(0.0))
            rowf[:, lanes] = high
            rowb[:, lanes] = high.astype(bf16)
        return carry

    lax.fori_loop(0, NOWN, build, 0)

    @pl.when(is_owner)
    def _():
        pl.semaphore_wait(barrier, NOWN)

    @pl.when(jnp.logical_not(is_owner))
    def _():
        pl.semaphore_wait(barrier, NOWN + 1)

    give = pltpu.make_async_remote_copy(
        src_ref=orb_hbm, dst_ref=prev, send_sem=orb_sem.at[0], recv_sem=orb_sem.at[1],
        device_id={"band": after}, device_id_type=MESH,
    )
    give.start()
    for load in loads:
        load.wait()

    def forward(pair, partner, then):
        density = (own[...] * partner[...]).reshape(2 * N, N)
        along = right_table(density, taby[...])
        planes = left_table(tabf[...], jnp.concatenate([along[:N], along[N:]], axis=1))
        half = N // 2
        rows = jnp.concatenate(
            [
                jnp.concatenate([planes[:half, :N], planes[half:, :N]], axis=1),
                jnp.concatenate([planes[:half, N:], planes[half:, N:]], axis=1),
            ],
            axis=0,
        )
        hi, lo = two_terms(rows)
        left = jnp.concatenate([hi, lo], axis=0)

        def step(g, carry):
            lanes = pl.ds(pl.multiple_of(g * LANES, LANES), LANES)
            picked = dot(left, pick[:, lanes])
            mask = rowf[:, lanes]
            for plane in range(2):
                a = plane * half
                both = (picked[a : a + half] + picked[N + a : N + a + half]) * mask
                total = jnp.sum(both, axis=0, keepdims=True)
                for i in range(PER):
                    for blk in range(2):
                        at = (2 * i + blk) * N
                        row = 4 * blk + 2 * pair + plane
                        send1[PER * g + i, row : row + 1, :] = total[:, at : at + N]
            if then is not None:
                for i in range(PER):
                    then(PER * g + i)
            return carry

        lax.fori_loop(0, STEPS, step, 0)

    forward(0, own, None)

    give.wait_recv()

    def out_copy(o):
        return pltpu.make_async_remote_copy(
            src_ref=send1.at[o], dst_ref=recv1.at[me], send_sem=out1_sem, recv_sem=in1_sem,
            device_id={"fft": owner_device(o)}, device_id_type=MESH,
        )

    def send_out(o):
        @pl.when(owner_device(o) != me)
        def _():
            out_copy(o).start()

    forward(1, prev, send_out)

    @pl.when(is_owner)
    def _():
        recv1[me] = send1[me]
        z_iota = signed(lax.broadcasted_iota(jnp.int32, (N, N), 0))
        weights = []
        for source in (me, partner_block(me)):
            flat = cols[pl.ds(source, 1), :]
            row = signed(lax.div(flat, N))
            col = signed(lax.rem(flat, N))
            weights.append(coulomb(z_iota * z_iota + (row * row + col * col)))
        pltpu.make_async_copy(recv1.at[pl.ds(0, NF - 1)], recv1.at[pl.ds(0, NF - 1)], in1_sem).wait()
        got = recv1.reshape(NF * 8, N)
        parts = []
        for q in range(0, 8, 2):
            parts.append(
                jnp.concatenate(
                    [got[pl.ds(q, NF, stride=8), :], got[pl.ds(q + 1, NF, stride=8), :]], axis=0
                )
            )
        spectral = left_table(tabi[...], jnp.concatenate(parts, axis=1))
        v = jnp.concatenate([weights[0], weights[0], weights[1], weights[1]], axis=1)
        weighted = v * spectral
        back = left_table(tabf[...], weighted)
        put = send2.reshape(NF * 8, N)
        for q in range(8):
            a = (q % 2) * NF
            put[pl.ds(q, NF, stride=8), :] = back[a : a + NF, (q // 2) * N : (q // 2 + 1) * N]

        def send_back(i, carry):
            peer = lax.rem(me + i, NF)
            pltpu.make_async_remote_copy(
                src_ref=send2.at[peer], dst_ref=recv2.at[me], send_sem=out2_sem,
                recv_sem=in2_sem.at[me // PER], device_id={"fft": peer}, device_id_type=MESH,
            ).start()
            return carry

        lax.fori_loop(1, NF, send_back, 0)
        recv2[me] = send2[me]
        energy = weighted * spectral
        en[...] = 0.5 * (energy[:, 2 * N : 3 * N] + energy[:, 3 * N :])
        en_copy = pltpu.make_async_remote_copy(
            src_ref=en, dst_ref=spec, send_sem=en_sem.at[0], recv_sem=en_sem.at[1],
            device_id={"fft": partner_block(me)}, device_id_type=MESH,
        )
        en_copy.start()
        spec[...] = 0.5 * (energy[:, :N] + energy[:, N : 2 * N])

    acc[...] = jnp.zeros_like(acc)

    def gather(g, carry):
        holds_me = is_owner & (me // PER == g)
        in_bytes = lambda n: pltpu.make_async_copy(
            recv2.at[pl.ds(0, n)], recv2.at[pl.ds(0, n)], in2_sem.at[g]
        )

        @pl.when(holds_me)
        def _():
            in_bytes(PER - 1).wait()

        @pl.when(jnp.logical_not(holds_me))
        def _():
            in_bytes(PER).wait()

        half = N // 2
        for i in range(PER):
            block = recv2[PER * g + i]
            hi = block.astype(bf16).astype(f32)
            lo = block - hi
            for blk in range(2):
                lanes = pl.ds(pl.multiple_of(g * LANES + (2 * i + blk) * N, N), N)
                mask = rowb[:, lanes].reshape(4, 16, N)
                at = (2 * i + blk) * N
                for term, part in enumerate((hi, lo)):
                    for r in range(4):
                        row = 4 * blk + r
                        one = jnp.broadcast_to(part[row : row + 1], (16, N)).astype(bf16)
                        a = term * 2 * N + r * half
                        wide[a : a + half, at : at + N] = (mask * one[None]).reshape(half, N)
        lanes = pl.ds(pl.multiple_of(g * LANES, LANES), LANES)
        both = lax.dot_general(
            wide[...], pick[:, lanes], (((1,), (1,)), ((), ())), preferred_element_type=f32
        )
        acc[...] += both[: 2 * N] + both[2 * N :]
        return carry

    lax.fori_loop(0, STEPS, gather, 0)

    half = N // 2
    total = None
    for pair, partner in enumerate((own, prev)):
        quarter = [
            [acc[(2 * pair + plane) * half : (2 * pair + plane + 1) * half, p * N : (p + 1) * N] for plane in range(2)]
            for p in range(2)
        ]
        freq = jnp.concatenate([jnp.concatenate(q, axis=1) for q in quarter], axis=0)
        rows = left_table(tabi[...], freq)
        pot = right_table(jnp.concatenate([rows[:, :N], rows[:, N:]], axis=0), taby[...])
        term = pot * partner[...].reshape(2 * N, N)
        total = term if total is None else total + term
    field[...] = (-total).reshape(2, N, N)

    give.wait_send()

    def sent(n, buf, sem):
        pltpu.make_async_copy(buf.at[pl.ds(0, n)], buf.at[pl.ds(0, n)], sem).wait()

    @pl.when(is_owner)
    def _():
        sent(NOWN - 1, send1, out1_sem)
        sent(NF - 1, send2, out2_sem)
        pltpu.make_async_copy(en, en, en_sem.at[0]).wait()

    @pl.when(jnp.logical_not(is_owner))
    def _():
        sent(NOWN, send1, out1_sem)
        pltpu.make_async_copy(en, en, en_sem.at[1]).wait()


def body(orbitals, stick_cols):
    along_y, split_rows, split_cols = tables()
    anywhere = pl.BlockSpec(memory_space=pl.ANY)
    vmem = pl.BlockSpec(memory_space=pltpu.VMEM)
    field, spec = pl.pallas_call(
        kernel,
        out_shape=(
            jax.ShapeDtypeStruct((2, N, N), f32),
            jax.ShapeDtypeStruct((N, N), f32),
        ),
        in_specs=[anywhere, vmem, anywhere, anywhere, anywhere],
        out_specs=(vmem, vmem),
        scratch_shapes=[
            pltpu.VMEM((2, N, N), f32),
            pltpu.VMEM((2, N, N), f32),
            pltpu.VMEM((2 * N, 2 * N), bf16),
            pltpu.VMEM((2 * N, 2 * N), bf16),
            pltpu.VMEM((2 * N, 2 * N), bf16),
            pltpu.VMEM((2 * N, NF * N), bf16),
            pltpu.VMEM((N // 2, NF * N), f32),
            pltpu.VMEM((N // 2, NF * N), bf16),
            pltpu.VMEM((NOWN, 8, N), f32),
            pltpu.VMEM((NF, 8, N), f32),
            pltpu.VMEM((NF, 8, N), f32),
            pltpu.VMEM((NOWN, 8, N), f32),
            pltpu.VMEM((4 * N, LANES), bf16),
            pltpu.VMEM((2 * N, 2 * N), f32),
            pltpu.VMEM((N, N), f32),
            pltpu.SemaphoreType.DMA((4,)),
            pltpu.SemaphoreType.DMA((2,)),
            pltpu.SemaphoreType.DMA,
            pltpu.SemaphoreType.DMA,
            pltpu.SemaphoreType.DMA,
            pltpu.SemaphoreType.DMA((STEPS,)),
            pltpu.SemaphoreType.DMA((2,)),
        ],
        compiler_params=pltpu.CompilerParams(
            collective_id=0, has_side_effects=True, vmem_limit_bytes=40 << 20
        ),
        name="exchange",
    )(
        orbitals.reshape(2, N, N),
        stick_cols.reshape(NF, N),
        jnp.asarray(along_y),
        jnp.asarray(split_rows),
        jnp.asarray(split_cols),
    )
    return field[None], spec[None]


def solution(mesh):
    return jax.shard_map(
        body,
        mesh=mesh,
        in_specs=(P("band", "fft", None, None), P()),
        out_specs=(P("band", "fft", None, None), P("band", None, "fft")),
        check_vma=False,
    )
```

time: 327 us -> 45.8 us (0.14)
  the two profiles are of different devices: /device:TPU:58 before, /device:TPU:1 now
where the time goes in v1:
time: 45.8 us; the launch traced here: 45.6 us
  Pallas kernels  39.3 us (86%)
  local copies, waits for them, and re-layouts  5.65 us (12%)
  between operations  0.65 us (1%)
    pallas_call x1, Pallas kernels, body(): pl.pallas_call(kernel, out_shape=(jax.ShapeDtypeStruct((2, N, N), f32), j...  39.3 us
    unnamed x12, local copies, waits for them, and re-layouts  5.65 us

profile of v1, /device:TPU:1, one launch (start us, length us, event | category | flops | bytes accessed | tf_op | source)
XLA Modules:
  0.0 45.6 jit_solution(1234486110186568121)
XLA Ops:
  0.6 0.0 copy-start
  0.6 0.9 %copy-done = f32[1,2,128,128]{3,2,1,0:T(8,128)S(1)} copy-done((f32[1,2,128,128]{3,2,1,0:T(8,128)S(1)}, f32[1,2,128,128]{3,2,1,0:T(8,128)}, u32[]{:S(2)}) %copy-start) | copy-done | bytes 131096
  1.5 0.0 copy-start.1
  1.5 0.9 %copy-done.1 = bf16[256,256]{1,0:T(8,128)(2,1)S(1)} copy-done((bf16[256,256]{1,0:T(8,128)(2,1)S(1)}, bf16[256,256]{1,0:T(8,128)(2,1)}, u32[]{:S(2)}) %copy-start.1) | copy-done | bytes 131096
  2.4 0.0 copy-start.2
  2.4 0.9 %copy-done.2 = bf16[256,256]{1,0:T(8,128)(2,1)S(1)} copy-done((bf16[256,256]{1,0:T(8,128)(2,1)S(1)}, bf16[256,256]{1,0:T(8,128)(2,1)}, u32[]{:S(2)}) %copy-start.2) | copy-done | bytes 131096
  3.3 0.0 copy-start.3
  3.3 0.9 %copy-done.3 = bf16[256,256]{1,0:T(8,128)(2,1)S(1)} copy-done((bf16[256,256]{1,0:T(8,128)(2,1)S(1)}, bf16[256,256]{1,0:T(8,128)(2,1)}, u32[]{:S(2)}) %copy-start.3) | copy-done | bytes 131096
  4.2 0.0 copy-start.4
  4.3 0.8 %copy-done.4 = s32[8192]{0:T(1024)S(1)} copy-done((s32[8192]{0:T(1024)S(1)}, s32[8192]{0:T(1024)}, u32[]{:S(2)}) %copy-start.4) | copy-done | bytes 32792
  5.0 39.3 %exchange.1 = (f32[2,128,128]{2,1,0:T(8,128)S(1)}, f32[128,128]{1,0:T(8,128)S(1)}) custom-call(f32[2,128,128]{2,1,0:T(8,128)S(1)} %bitcast.4, s32[64,128]{1,0:T(8,128)S(1)} %bitcast.7, bf16[256,256]{1,0:T(8,128)(2,1)S(1)} %copy-done.3, bf16[256,256]{1,0:T(8,128)(2,1)S(1)} %copy-done.2, bf16[256,256]{1,0:T(8,128)(2,1)S(1)} %copy-done.1), custom_call_target="tpu_custom_call" | custom-call | tf_op jit(solution)/shard_map/exchange/pallas_call | solution.py:323
  44.3 0.7 %copy.9 = f32[1,2,128,128]{3,2,1,0:T(8,128)} copy(f32[1,2,128,128]{3,2,1,0:T(8,128)S(1)} %bitcast.5) | data formatting | bytes 262144
  45.0 0.6 %copy.10 = f32[1,128,128]{2,1,0:T(8,128)} copy(f32[1,128,128]{2,1,0:T(8,128)S(1)} %bitcast.6) | data formatting | bytes 131072
Async XLA Ops:
  0.6 0.9 %copy-start = (f32[1,2,128,128]{3,2,1,0:T(8,128)S(1)}, f32[1,2,128,128]{3,2,1,0:T(8,128)}, u32[]{:S(2)}) copy-start(f32[1,2,128,128]{3,2,1,0:T(8,128)} %param.5) | copy-start | bytes 393220
  1.5 0.9 %copy-start.1 = (bf16[256,256]{1,0:T(8,128)(2,1)S(1)}, bf16[256,256]{1,0:T(8,128)(2,1)}, u32[]{:S(2)}) copy-start(bf16[256,256]{1,0:T(8,128)(2,1)} %constant.8.clone.tabi_hbm) | copy-start | bytes 393220
  2.4 0.9 %copy-start.2 = (bf16[256,256]{1,0:T(8,128)(2,1)S(1)}, bf16[256,256]{1,0:T(8,128)(2,1)}, u32[]{:S(2)}) copy-start(bf16[256,256]{1,0:T(8,128)(2,1)} %constant.7.clone.tabf_hbm) | copy-start | bytes 393220
  3.3 0.9 %copy-start.3 = (bf16[256,256]{1,0:T(8,128)(2,1)S(1)}, bf16[256,256]{1,0:T(8,128)(2,1)}, u32[]{:S(2)}) copy-start(bf16[256,256]{1,0:T(8,128)(2,1)} %constant.6.clone.taby_hbm) | copy-start | bytes 393220
  4.2 0.8 %copy-start.4 = (s32[8192]{0:T(1024)S(1)}, s32[8192]{0:T(1024)}, u32[]{:S(2)}) copy-start(s32[8192]{0:T(1024)} %param.6) | copy-start | bytes 98308

commit v2 on v1

v2 whole, which is shorter than its diff:
```python
import functools
import math

import jax
import jax.numpy as jnp
import ml_dtypes
import numpy as np
from jax import lax
from jax.experimental import pallas as pl
from jax.experimental.pallas import tpu as pltpu
from jax.sharding import PartitionSpec as P

RAD = 48
N = 128
NF = 64
NBAND = 4
NOWN = 32
PER = 4
STEPS = NOWN // PER
LANES = PER * 2 * N
TILES = 5
ROWS = 8 * TILES

screening = 16.0
strength = 10.0

MESH = pl.DeviceIdType.MESH
f32 = jnp.float32
bf16 = jnp.bfloat16


def owner_device(o):
    return o // 2 * 4 + o % 2


def owner_index(f):
    return f // 4 * 2 + f % 4


def owns(f):
    return f % 4 < 2


def partner_block(o):
    return o // 2 * 4 + 3 - o % 2


def back_step(me, i):
    t = (i + 1) // 2
    return (me // 8 + t * (1 - 2 * (i % 2)) + 8) % 8


def tables():
    k = np.arange(N)
    angles = 2.0 * math.pi / N * (k[:, None] * k[None, :] % N)
    c = (np.cos(angles) + np.sin(angles)) / math.sqrt(N)

    def terms(x):
        hi = x.astype(np.float32).astype(ml_dtypes.bfloat16)
        lo = (x - hi.astype(np.float64)).astype(np.float32).astype(ml_dtypes.bfloat16)
        return hi, lo

    def left(x):
        hi, lo = terms(x)
        return np.block([[hi, hi], [lo, lo]])

    def right(x):
        hi, lo = terms(x)
        return np.block([[hi, lo], [hi, lo]])

    by_b = np.zeros((N, N))
    by_b[:, : 2 * RAD + 1] = c[:, (np.arange(2 * RAD + 1) - RAD) % N]
    by_a = np.zeros((N, N))
    for sub in range(8):
        for t in range(16):
            index = 8 * t + sub if t < 12 else 8 * (t - 4) + sub
            if sub == 7 and t >= 12:
                index = 2 * RAD if t == 15 else None
            if index is not None:
                by_a[16 * sub + t] = c[(index - RAD) % N]
    order = np.concatenate([k[0::2], k[1::2]])
    return np.stack(
        [right(by_b), left(by_a), left(c[:, order]), left(c[order]), left(by_a.T), right(by_b.T)]
    )


def two_terms(x):
    hi = x.astype(bf16)
    return hi, (x - hi.astype(f32)).astype(bf16)


def signed(x):
    return jnp.where(x < N // 2, x, x - N)


def coulomb(squared):
    kappa = squared.astype(f32)
    safe = jnp.maximum(kappa, f32(1.0))
    values = strength * screening * (1.0 - jnp.exp(-kappa / screening)) / safe
    inside = (squared > 0) & (squared <= RAD * RAD)
    return jnp.where(inside, values, f32(0.0))


def dot(a, b):
    return jnp.dot(a, b, preferred_element_type=f32)


def left_table(table, x):
    hi, lo = two_terms(x)
    both = dot(table, jnp.concatenate([hi, lo], axis=0))
    return both[:N] + both[N:]


def right_table(x, table):
    hi, lo = two_terms(x)
    both = dot(jnp.concatenate([hi, lo], axis=1), table)
    return both[:, :N] + both[:, N:]


def turn(x, groups):
    return x if groups % 4 == 0 else pltpu.roll(x, groups % 4 * 32, axis=1)


def masks():
    group = lax.broadcasted_iota(jnp.int32, (8, N), 1) // 32
    row = lax.broadcasted_iota(jnp.int32, (8, N), 0)
    return [group == i for i in range(4)], row < 4, row == 7


def by_group(groups, parts):
    low = jnp.where(groups[0], parts[0], parts[1])
    high = jnp.where(groups[2], parts[2], parts[3])
    return jnp.where(groups[0] | groups[1], low, high)


def pack(plane):
    groups, upper, last = masks()
    tiles = [[], [], [], [], []]
    for h in range(2):
        parts = [[], [], [], [], []]
        for i in range(4):
            sub = 4 * h + i
            main = plane[16 * sub : 16 * sub + 8]
            rest = plane[16 * sub + 8 : 16 * sub + 16]
            for y in range(3):
                parts[y].append(turn(main, i - y))
            second = turn(rest, i - 1)
            moved = pltpu.roll(second, 4, axis=0) if sub == 7 else second
            parts[3].append(jnp.where(upper, turn(rest, i), moved))
            third = turn(rest, i - 2)
            if sub == 0:
                third = jnp.where(upper, third, turn(main, i - 3))
            if sub == 7:
                third = jnp.where(last, second, third)
            parts[4].append(third)
        for t in range(TILES):
            tiles[t].append(by_group(groups, parts[t]))
    return [jnp.concatenate(t, axis=1) for t in tiles]


def unpack(tiles):
    groups, upper, last = masks()
    zero = jnp.zeros((8, N), f32)
    out = []
    for sub in range(8):
        h, i = sub // 4, sub % 4
        t0, t1, t2, t3, t4 = (t[:, h * N : (h + 1) * N] for t in tiles)
        special = zero
        if sub == 0:
            special = jnp.where(upper, zero, turn(t4, 3 - i))
        out.append(by_group(groups, [turn(t0, -i), turn(t1, 1 - i), turn(t2, 2 - i), special]))
        first = jnp.where(upper, turn(t3, -i), zero)
        third = jnp.where(upper, turn(t4, 2 - i), zero)
        second = turn(t3, 1 - i)
        if sub == 7:
            second = jnp.where(
                upper, pltpu.roll(second, 4, axis=0), jnp.where(last, turn(t4, 1 - i), zero)
            )
        else:
            second = jnp.where(upper, zero, second)
        out.append(by_group(groups, [first, second, third, zero]))
    return jnp.concatenate(out, axis=0)


def kernel(
    orb_hbm, cols_hbm, tab_hbm, field, spec,
    cols, places, lanes_of, own, prev, tab, pick, rowf, rowb, send1, recv1, send2, recv2, wide, acc, en,
    load_sem, orb_sem, out1_sem, in1_sem, out2_sem, in2_sem, en_sem,
):
    me = lax.axis_index("fft")
    band = lax.axis_index("band")
    is_owner = owns(me)
    mine = owner_index(me)
    before = lax.rem(band + NBAND - 1, NBAND)
    after = lax.rem(band + 1, NBAND)

    loads = [
        pltpu.make_async_copy(src, dst, load_sem.at[i])
        for i, (src, dst) in enumerate(((cols_hbm, cols), (orb_hbm, own), (tab_hbm, tab)))
    ]
    y_to, x_to, z_to, z_from, x_from, y_from = (tab.at[i] for i in range(6))
    for load in loads:
        load.start()

    barrier = pltpu.get_barrier_semaphore()
    pl.semaphore_signal(barrier, inc=1, device_id={"band": before}, device_id_type=MESH)

    @pl.when(is_owner)
    def _():
        def greet(i, carry):
            pl.semaphore_signal(
                barrier, inc=1, device_id={"fft": lax.rem(me + i, NF)}, device_id_type=MESH
            )
            return carry

        lax.fori_loop(1, NF, greet, 0)

    loads[0].wait()
    flat = cols[...]
    along_a = signed(lax.div(flat, N)) + RAD
    along_b = signed(lax.rem(flat, N)) + RAD
    inside = (along_a >= 0) & (along_a < 2 * RAD) & (along_b >= 0) & (along_b < 2 * RAD)
    big_a, big_b = along_a >> 3, along_b >> 5
    row = jnp.where(big_a < 8, 8 * big_b + big_a, 16 + 4 * big_b + big_a)
    row = jnp.where(inside, row, -1)
    lane = 32 * (along_a & 7) + (along_b & 31)
    top = (along_a == RAD) & (along_b == 2 * RAD)
    side = (along_a == 2 * RAD) & (along_b == RAD)
    places[...] = jnp.where(top, 38, jnp.where(side, 39, row))
    lanes_of[...] = jnp.where(top, 0, jnp.where(side, 240, lane))
    low_iota = lax.broadcasted_iota(jnp.int32, (2 * N, N), 0)
    row_iota = lax.broadcasted_iota(jnp.int32, (ROWS, N), 0)
    twice = lax.broadcasted_iota(jnp.int32, (2 * ROWS, N), 0)
    twice = 8 * lax.div(twice, 16) + lax.rem(twice, 8)

    def build(o):
        for blk, source in enumerate((owner_device(o), partner_block(o))):
            place = places[pl.ds(source, 1), :]
            lanes = pl.ds(pl.multiple_of((2 * o + blk) * N, N), N)
            pick[:, lanes] = jnp.where(low_iota == lanes_of[pl.ds(source, 1), :], 1.0, 0.0).astype(bf16)
            rowf[:, lanes] = jnp.where(row_iota == place, f32(1.0), f32(0.0))
            rowb[:, lanes] = jnp.where(twice == place, 1.0, 0.0).astype(bf16)

    lax.fori_loop(0, NOWN, lambda o, c: (build(o), c)[1], 0)

    @pl.when(is_owner)
    def _():
        pl.semaphore_wait(barrier, NOWN)

    @pl.when(jnp.logical_not(is_owner))
    def _():
        pl.semaphore_wait(barrier, NOWN + 1)

    give = pltpu.make_async_remote_copy(
        src_ref=orb_hbm, dst_ref=prev, send_sem=orb_sem.at[0], recv_sem=orb_sem.at[1],
        device_id={"band": after}, device_id_type=MESH,
    )
    give.start()

    for load in loads[1:]:
        load.wait()

    def forward(pair, partner, then):
        density = (own[...] * partner[...]).reshape(2 * N, N)
        along = right_table(density, y_to[...])
        planes = left_table(x_to[...], jnp.concatenate([along[:N], along[N:]], axis=1))
        packed = [pack(planes[:, :N]), pack(planes[:, N:])]
        rows = jnp.concatenate([packed[p][t] for t in range(TILES) for p in range(2)], axis=0)
        hi, lo = two_terms(rows)
        left = jnp.concatenate([hi, lo], axis=0)

        def step(i, carry):
            g = STEPS - 1 - i
            lanes = pl.ds(pl.multiple_of(g * LANES, LANES), LANES)
            picked = dot(left, pick[:, lanes])
            for plane in range(2):
                sums = None
                for t in range(TILES):
                    a = 16 * t + 8 * plane
                    both = picked[a : a + 8] + picked[2 * ROWS + a : 2 * ROWS + a + 8]
                    both = both * rowf[8 * t : 8 * t + 8, lanes]
                    sums = both if sums is None else sums + both
                total = jnp.sum(sums, axis=0, keepdims=True)
                for i in range(PER):
                    for blk in range(2):
                        at = (2 * i + blk) * N
                        row = 4 * blk + 2 * pair + plane
                        send1[PER * g + i, row : row + 1, :] = total[:, at : at + N]
            if then is not None:
                for i in range(PER):
                    then(PER * g + i)
            return carry

        lax.fori_loop(0, STEPS, step, 0)

    forward(0, own, None)

    give.wait_recv()

    def out_copy(o):
        return pltpu.make_async_remote_copy(
            src_ref=send1.at[o], dst_ref=recv1.at[me], send_sem=out1_sem, recv_sem=in1_sem,
            device_id={"fft": owner_device(o)}, device_id_type=MESH,
        )

    def send_out(o):
        @pl.when(owner_device(o) != me)
        def _():
            out_copy(o).start()

    forward(1, prev, send_out)

    @pl.when(is_owner)
    def _():
        recv1[me] = send1[mine]
        z_iota = signed(lax.broadcasted_iota(jnp.int32, (N, N), 0))
        weights = []
        for source in (me, partner_block(mine)):
            flat = cols[pl.ds(source, 1), :]
            row = signed(lax.div(flat, N))
            col = signed(lax.rem(flat, N))
            weights.append(coulomb(z_iota * z_iota + (row * row + col * col)))
        pltpu.make_async_copy(recv1.at[pl.ds(0, NF - 1)], recv1.at[pl.ds(0, NF - 1)], in1_sem).wait()
        got = recv1.reshape(NF * 8, N)
        parts = []
        for q in range(0, 8, 2):
            parts.append(
                jnp.concatenate(
                    [got[pl.ds(q, NF, stride=8), :], got[pl.ds(q + 1, NF, stride=8), :]], axis=0
                )
            )
        spectral = left_table(z_to[...], jnp.concatenate(parts, axis=1))
        v = jnp.concatenate([weights[0], weights[0], weights[1], weights[1]], axis=1)
        weighted = v * spectral
        back = left_table(z_from[...], weighted)
        put = send2.reshape(NF * 8, N)
        for q in range(8):
            a = (q % 2) * NF
            put[pl.ds(q, NF, stride=8), :] = back[a : a + NF, (q // 2) * N : (q // 2 + 1) * N]

        def send_back(z, carry):
            for k in range(8):
                peer = z * 8 + k

                @pl.when(peer != me)
                def _():
                    pltpu.make_async_remote_copy(
                        src_ref=send2.at[peer], dst_ref=recv2.at[mine], send_sem=out2_sem,
                        recv_sem=in2_sem.at[mine // PER], device_id={"fft": peer},
                        device_id_type=MESH,
                    ).start()

            return carry

        lax.fori_loop(0, NF // 8, send_back, 0)
        recv2[mine] = send2[me]
        energy = weighted * spectral
        en[...] = 0.5 * (energy[:, 2 * N : 3 * N] + energy[:, 3 * N :])
        en_copy = pltpu.make_async_remote_copy(
            src_ref=en, dst_ref=spec, send_sem=en_sem.at[0], recv_sem=en_sem.at[1],
            device_id={"fft": partner_block(mine)}, device_id_type=MESH,
        )
        en_copy.start()
        spec[...] = 0.5 * (energy[:, :N] + energy[:, N : 2 * N])

    acc[...] = jnp.zeros_like(acc)

    def gather(i, carry):
        g = back_step(me, i)
        holds_me = is_owner & (mine // PER == g)
        in_bytes = lambda n: pltpu.make_async_copy(
            recv2.at[pl.ds(0, n)], recv2.at[pl.ds(0, n)], in2_sem.at[g]
        )

        @pl.when(holds_me)
        def _():
            in_bytes(PER - 1).wait()

        @pl.when(jnp.logical_not(holds_me))
        def _():
            in_bytes(PER).wait()

        for i in range(PER):
            block = recv2[PER * g + i]
            hi = block.astype(bf16).astype(f32)
            lo = block - hi
            for blk in range(2):
                lanes = pl.ds(pl.multiple_of(g * LANES + (2 * i + blk) * N, N), N)
                at = (2 * i + blk) * N
                for term, part in enumerate((hi, lo)):
                    for r in range(0, 4, 2):
                        row = 4 * blk + r
                        two = [jnp.broadcast_to(part[q : q + 1], (8, N)) for q in (row, row + 1)]
                        one = jnp.concatenate(two, axis=0).astype(bf16)
                        for t in range(TILES):
                            a = term * 4 * ROWS + 32 * t + 8 * r
                            wide[a : a + 16, at : at + N] = rowb[16 * t : 16 * t + 16, lanes] * one
        lanes = pl.ds(pl.multiple_of(g * LANES, LANES), LANES)
        both = lax.dot_general(
            wide[...], pick[:, lanes], (((1,), (1,)), ((), ())), preferred_element_type=f32
        )
        acc[...] += both[: 4 * ROWS] + both[4 * ROWS :]
        return carry

    lax.fori_loop(0, STEPS, gather, 0)

    total = None
    for pair, partner in enumerate((own, prev)):
        freq = jnp.concatenate(
            [
                unpack([acc[32 * t + 8 * r : 32 * t + 8 * r + 8, :] for t in range(TILES)])
                for r in (2 * pair, 2 * pair + 1)
            ],
            axis=1,
        )
        rows = left_table(x_from[...], freq)
        pot = right_table(jnp.concatenate([rows[:, :N], rows[:, N:]], axis=0), y_from[...])
        term = pot * partner[...].reshape(2 * N, N)
        total = term if total is None else total + term
    field[...] = (-total).reshape(2, N, N)

    give.wait_send()

    def sent(n, buf, sem):
        pltpu.make_async_copy(buf.at[pl.ds(0, n)], buf.at[pl.ds(0, n)], sem).wait()

    @pl.when(is_owner)
    def _():
        sent(NOWN - 1, send1, out1_sem)
        sent(NF - 1, send2, out2_sem)
        pltpu.make_async_copy(en, en, en_sem.at[0]).wait()

    @pl.when(jnp.logical_not(is_owner))
    def _():
        sent(NOWN, send1, out1_sem)
        pltpu.make_async_copy(en, en, en_sem.at[1]).wait()


def body(orbitals, stick_cols):
    anywhere = pl.BlockSpec(memory_space=pltpu.HBM)
    vmem = pl.BlockSpec(memory_space=pltpu.VMEM)
    field, spec = pl.pallas_call(
        kernel,
        out_shape=(
            jax.ShapeDtypeStruct((2, N, N), f32),
            jax.ShapeDtypeStruct((N, N), f32),
        ),
        in_specs=[anywhere] * 3,
        out_specs=(vmem, vmem),
        scratch_shapes=[
            pltpu.VMEM((NF, N), jnp.int32),
            pltpu.VMEM((NF, N), jnp.int32),
            pltpu.VMEM((NF, N), jnp.int32),
            pltpu.VMEM((2, N, N), f32),
            pltpu.VMEM((2, N, N), f32),
            pltpu.VMEM((6, 2 * N, 2 * N), bf16),
            pltpu.VMEM((2 * N, NF * N), bf16),
            pltpu.VMEM((ROWS, NF * N), f32),
            pltpu.VMEM((2 * ROWS, NF * N), bf16),
            pltpu.VMEM((NOWN, 8, N), f32),
            pltpu.VMEM((NF, 8, N), f32),
            pltpu.VMEM((NF, 8, N), f32),
            pltpu.VMEM((NOWN, 8, N), f32),
            pltpu.VMEM((8 * ROWS, LANES), bf16),
            pltpu.VMEM((4 * ROWS, 2 * N), f32),
            pltpu.VMEM((N, N), f32),
            pltpu.SemaphoreType.DMA((3,)),
            pltpu.SemaphoreType.DMA((2,)),
            pltpu.SemaphoreType.DMA,
            pltpu.SemaphoreType.DMA,
            pltpu.SemaphoreType.DMA,
            pltpu.SemaphoreType.DMA((STEPS,)),
            pltpu.SemaphoreType.DMA((2,)),
        ],
        compiler_params=pltpu.CompilerParams(
            collective_id=0, has_side_effects=True, vmem_limit_bytes=(64 << 20) - (10615 << 10)
        ),
        name="exchange",
    )(
        orbitals.reshape(2, N, N),
        stick_cols.reshape(NF, N),
        jnp.asarray(tables()),
    )
    return field[None], spec[None]


def solution(mesh):
    return jax.shard_map(
        body,
        mesh=mesh,
        in_specs=(P("band", "fft", None, None), P()),
        out_specs=(P("band", "fft", None, None), P("band", None, "fft")),
        check_vma=False,
    )
```

time: 45.8 us -> 35.7 us (0.78)
  the two profiles are of different devices: /device:TPU:1 before, /device:TPU:58 now
where the time goes in v2:
time: 35.7 us; the launch traced here: 35.3 us
  Pallas kernels  32.6 us (91%)
  local copies, waits for them, and re-layouts  2.04 us (6%)
  between operations  0.65 us (2%)
    pallas_call x1, Pallas kernels, body(): pl.pallas_call(kernel, out_shape=(jax.ShapeDtypeStruct((2, N, N), f32), j...  32.6 us
    unnamed x4, local copies, waits for them, and re-layouts  2.04 us

profile of v2, /device:TPU:58, one launch (start us, length us, event | category | flops | bytes accessed | tf_op | source)
XLA Modules:
  0.0 35.3 jit_solution(15923257619971397643)
XLA Ops:
  0.6 0.0 copy-start
  0.6 0.7 %copy-done = s32[8192]{0:T(1024)S(1)} copy-done((s32[8192]{0:T(1024)S(1)}, s32[8192]{0:T(1024)}, u32[]{:S(2)}) %copy-start) | copy-done | bytes 32792
  1.4 32.6 %exchange.1 = (f32[2,128,128]{2,1,0:T(8,128)S(1)}, f32[128,128]{1,0:T(8,128)S(1)}) custom-call(f32[2,128,128]{2,1,0:T(8,128)} %bitcast.7, s32[64,128]{1,0:T(8,128)S(1)} %bitcast.6, bf16[6,256,256]{2,1,0:T(8,128)(2,1)} %constant.2.clone.tab_hbm), custom_call_target="tpu_custom_call" | custom-call | tf_op jit(solution)/shard_map/exchange/pallas_call | solution.py:442
  34.0 0.7 %copy.7 = f32[1,2,128,128]{3,2,1,0:T(8,128)} copy(f32[1,2,128,128]{3,2,1,0:T(8,128)S(1)} %bitcast.4) | data formatting | bytes 262144
  34.6 0.6 %copy.8 = f32[1,128,128]{2,1,0:T(8,128)} copy(f32[1,128,128]{2,1,0:T(8,128)S(1)} %bitcast.5) | data formatting | bytes 131072
Async XLA Ops:
  0.6 0.8 %copy-start = (s32[8192]{0:T(1024)S(1)}, s32[8192]{0:T(1024)}, u32[]{:S(2)}) copy-start(s32[8192]{0:T(1024)} %param.4) | copy-start | bytes 98308

commit v3 on v2

--- a/solution.py
+++ b/solution.py
@@ -15,7 +15,7 @@
 NF = 64
 NBAND = 4
 NOWN = 32
-PER = 4
+PER = 8
 STEPS = NOWN // PER
 LANES = PER * 2 * N
 TILES = 5
@@ -47,7 +47,7 @@
 
 def back_step(me, i):
     t = (i + 1) // 2
-    return (me // 8 + t * (1 - 2 * (i % 2)) + 8) % 8
+    return (me // 16 + t * (1 - 2 * (i % 2)) + 4) % 4
 
 
 def tables():
@@ -194,6 +194,24 @@
     before = lax.rem(band + NBAND - 1, NBAND)
     after = lax.rem(band + 1, NBAND)
 
+    barrier = pltpu.get_barrier_semaphore()
+    pl.semaphore_signal(barrier, inc=1, device_id={"band": before}, device_id_type=MESH)
+
+    @pl.when(is_owner)
+    def _():
+        def greet(z, carry):
+            for k in range(8):
+
+                @pl.when(z * 8 + k != me)
+                def _():
+                    pl.semaphore_signal(
+                        barrier, inc=1, device_id={"fft": z * 8 + k}, device_id_type=MESH
+                    )
+
+            return carry
+
+        lax.fori_loop(0, NF // 8, greet, 0)
+
     loads = [
         pltpu.make_async_copy(src, dst, load_sem.at[i])
         for i, (src, dst) in enumerate(((cols_hbm, cols), (orb_hbm, own), (tab_hbm, tab)))
@@ -201,19 +219,6 @@
     y_to, x_to, z_to, z_from, x_from, y_from = (tab.at[i] for i in range(6))
     for load in loads:
         load.start()
-
-    barrier = pltpu.get_barrier_semaphore()
-    pl.semaphore_signal(barrier, inc=1, device_id={"band": before}, device_id_type=MESH)
-
-    @pl.when(is_owner)
-    def _():
-        def greet(i, carry):
-            pl.semaphore_signal(
-                barrier, inc=1, device_id={"fft": lax.rem(me + i, NF)}, device_id_type=MESH
-            )
-            return carry
-
-        lax.fori_loop(1, NF, greet, 0)
 
     loads[0].wait()
     flat = cols[...]
@@ -252,13 +257,13 @@
         pl.semaphore_wait(barrier, NOWN + 1)
 
     give = pltpu.make_async_remote_copy(
-        src_ref=orb_hbm, dst_ref=prev, send_sem=orb_sem.at[0], recv_sem=orb_sem.at[1],
+        src_ref=own, dst_ref=prev, send_sem=orb_sem.at[0], recv_sem=orb_sem.at[1],
         device_id={"band": after}, device_id_type=MESH,
     )
+    loads[1].wait()
     give.start()
 
-    for load in loads[1:]:
-        load.wait()
+    loads[2].wait()
 
     def forward(pair, partner, then):
         density = (own[...] * partner[...]).reshape(2 * N, N)
@@ -473,13 +478,13 @@
             pltpu.SemaphoreType.DMA((2,)),
         ],
         compiler_params=pltpu.CompilerParams(
-            collective_id=0, has_side_effects=True, vmem_limit_bytes=(64 << 20) - (10615 << 10)
+            collective_id=0, has_side_effects=True, vmem_limit_bytes=40 << 20
         ),
         name="exchange",
     )(
-        orbitals.reshape(2, N, N),
-        stick_cols.reshape(NF, N),
-        jnp.asarray(tables()),
+        pltpu.with_memory_space_constraint(orbitals.reshape(2, N, N), pltpu.HBM),
+        pltpu.with_memory_space_constraint(stick_cols.reshape(NF, N), pltpu.HBM),
+        pltpu.with_memory_space_constraint(jnp.asarray(tables()), pltpu.HBM),
     )
     return field[None], spec[None]
 

time: 35.7 us -> 33.7 us (0.944)
  Pallas kernels: 32.6 us -> 31.6 us
  local copies, waits for them, and re-layouts: 2.04 us -> 1.29 us
    pallas_call x1, Pallas kernels: 32.6 us -> 31.6 us  [body(): pl.pallas_call(kernel, out_shape=(jax.ShapeDtypeStruct((2, N, N), f32), j...]
    unnamed x4 -> x2, local copies, waits for them, and re-layouts: 2.04 us -> 1.29 us
where the time goes in v3:
time: 33.7 us; the launch traced here: 33.5 us
  Pallas kernels  31.6 us (94%)
  local copies, waits for them, and re-layouts  1.29 us (4%)
  between operations  0.64 us (2%)
    pallas_call x1, Pallas kernels, body(): pl.pallas_call(kernel, out_shape=(jax.ShapeDtypeStruct((2, N, N), f32), j...  31.6 us
    unnamed x2, local copies, waits for them, and re-layouts  1.29 us

profile of v3, /device:TPU:58, one launch (start us, length us, event | category | flops | bytes accessed | tf_op | source)
XLA Modules:
  0.0 33.5 jit_solution(7749658333983454962)
XLA Ops:
  0.6 31.6 %exchange.1 = (f32[2,128,128]{2,1,0:T(8,128)S(1)}, f32[128,128]{1,0:T(8,128)S(1)}) custom-call(f32[2,128,128]{2,1,0:T(8,128)} %bitcast.6, s32[64,128]{1,0:T(8,128)} %bitcast.7, bf16[6,256,256]{2,1,0:T(8,128)(2,1)} %constant.2.clone.tab_hbm), custom_call_target="tpu_custom_call" | custom-call | tf_op jit(solution)/shard_map/exchange/pallas_call | solution.py:447
  32.2 0.7 %copy.7 = f32[1,2,128,128]{3,2,1,0:T(8,128)} copy(f32[1,2,128,128]{3,2,1,0:T(8,128)S(1)} %bitcast.4) | data formatting | bytes 262144
  32.9 0.6 %copy.8 = f32[1,128,128]{2,1,0:T(8,128)} copy(f32[1,128,128]{2,1,0:T(8,128)S(1)} %bitcast.5) | data formatting | bytes 131072

commit v4 on v3

--- a/solution.py
+++ b/solution.py
@@ -345,7 +345,7 @@
 
         def send_back(z, carry):
             for k in range(8):
-                peer = z * 8 + k
+                peer = z * 8 + (k + 4 * (band % 2)) % 8
 
                 @pl.when(peer != me)
                 def _():
@@ -409,19 +409,15 @@
 
     lax.fori_loop(0, STEPS, gather, 0)
 
-    total = None
-    for pair, partner in enumerate((own, prev)):
-        freq = jnp.concatenate(
-            [
-                unpack([acc[32 * t + 8 * r : 32 * t + 8 * r + 8, :] for t in range(TILES)])
-                for r in (2 * pair, 2 * pair + 1)
-            ],
-            axis=1,
-        )
-        rows = left_table(x_from[...], freq)
-        pot = right_table(jnp.concatenate([rows[:, :N], rows[:, N:]], axis=0), y_from[...])
-        term = pot * partner[...].reshape(2 * N, N)
-        total = term if total is None else total + term
+    freq = jnp.concatenate(
+        [unpack([acc[32 * t + 8 * r : 32 * t + 8 * r + 8, :] for t in range(TILES)]) for r in range(4)],
+        axis=1,
+    )
+    rows = left_table(x_from[...], freq)
+    pot = right_table(
+        jnp.concatenate([rows[:, r * N : (r + 1) * N] for r in range(4)], axis=0), y_from[...]
+    )
+    total = pot[: 2 * N] * own[...].reshape(2 * N, N) + pot[2 * N :] * prev[...].reshape(2 * N, N)
     field[...] = (-total).reshape(2, N, N)
 
     give.wait_send()

time: 33.7 us -> 33.6 us (level); the launches traced: 33.5 us -> 33.1 us
  Pallas kernels: 31.6 us -> 31.1 us
    pallas_call x1, Pallas kernels: 31.6 us -> 31.1 us  [body(): pl.pallas_call(kernel, out_shape=(jax.ShapeDtypeStruct((2, N, N), f32), j...]
where the time goes in v4:
time: 33.6 us; the launch traced here: 33.1 us
  Pallas kernels  31.1 us (93%)
  local copies, waits for them, and re-layouts  1.29 us (4%)
  between operations  0.64 us (2%)
    pallas_call x1, Pallas kernels, body(): pl.pallas_call(kernel, out_shape=(jax.ShapeDtypeStruct((2, N, N), f32), j...  31.1 us
    unnamed x2, local copies, waits for them, and re-layouts  1.29 us

profile of v4, /device:TPU:58, one launch (start us, length us, event | category | flops | bytes accessed | tf_op | source)
XLA Modules:
  0.0 33.1 jit_solution(15260606537836929965)
XLA Ops:
  0.6 31.1 %exchange.1 = (f32[2,128,128]{2,1,0:T(8,128)S(1)}, f32[128,128]{1,0:T(8,128)S(1)}) custom-call(f32[2,128,128]{2,1,0:T(8,128)} %bitcast.6, s32[64,128]{1,0:T(8,128)} %bitcast.7, bf16[6,256,256]{2,1,0:T(8,128)(2,1)} %constant.2.clone.tab_hbm), custom_call_target="tpu_custom_call" | custom-call | tf_op jit(solution)/shard_map/exchange/pallas_call | solution.py:443
  31.8 0.7 %copy.7 = f32[1,2,128,128]{3,2,1,0:T(8,128)} copy(f32[1,2,128,128]{3,2,1,0:T(8,128)S(1)} %bitcast.4) | data formatting | bytes 262144
  32.4 0.6 %copy.8 = f32[1,128,128]{2,1,0:T(8,128)} copy(f32[1,128,128]{2,1,0:T(8,128)S(1)} %bitcast.5) | data formatting | bytes 131072

commit v5 on v4

--- a/solution.py
+++ b/solution.py
@@ -248,21 +248,7 @@
 
     lax.fori_loop(0, NOWN, lambda o, c: (build(o), c)[1], 0)
 
-    @pl.when(is_owner)
-    def _():
-        pl.semaphore_wait(barrier, NOWN)
-
-    @pl.when(jnp.logical_not(is_owner))
-    def _():
-        pl.semaphore_wait(barrier, NOWN + 1)
-
-    give = pltpu.make_async_remote_copy(
-        src_ref=own, dst_ref=prev, send_sem=orb_sem.at[0], recv_sem=orb_sem.at[1],
-        device_id={"band": after}, device_id_type=MESH,
-    )
     loads[1].wait()
-    give.start()
-
     loads[2].wait()
 
     def forward(pair, partner, then):
@@ -299,6 +285,21 @@
         lax.fori_loop(0, STEPS, step, 0)
 
     forward(0, own, None)
+
+    @pl.when(is_owner)
+    def _():
+        pl.semaphore_wait(barrier, NOWN)
+
+    @pl.when(jnp.logical_not(is_owner))
+    def _():
+        pl.semaphore_wait(barrier, NOWN + 1)
+
+    give = pltpu.make_async_remote_copy(
+        src_ref=own, dst_ref=prev, send_sem=orb_sem.at[0], recv_sem=orb_sem.at[1],
+        device_id={"band": after}, device_id_type=MESH,
+    )
+    give.start()
+
 
     give.wait_recv()
 

time: 33.6 us -> 33.6 us (level); the launches traced: 33.1 us -> 33.5 us
  Pallas kernels: 31.1 us -> 31.6 us
    pallas_call x1, Pallas kernels: 31.1 us -> 31.6 us  [body(): pl.pallas_call(kernel, out_shape=(jax.ShapeDtypeStruct((2, N, N), f32), j...]
where the time goes in v5:
time: 33.6 us; the launch traced here: 33.5 us
  Pallas kernels  31.6 us (94%)
  local copies, waits for them, and re-layouts  1.29 us (4%)
  between operations  0.64 us (2%)
    pallas_call x1, Pallas kernels, body(): pl.pallas_call(kernel, out_shape=(jax.ShapeDtypeStruct((2, N, N), f32), j...  31.6 us
    unnamed x2, local copies, waits for them, and re-layouts  1.29 us

profile of v5, /device:TPU:58, one launch (start us, length us, event | category | flops | bytes accessed | tf_op | source)
XLA Modules:
  0.0 33.5 jit_solution(5400890615768271892)
XLA Ops:
  0.6 31.6 %exchange.1 = (f32[2,128,128]{2,1,0:T(8,128)S(1)}, f32[128,128]{1,0:T(8,128)S(1)}) custom-call(f32[2,128,128]{2,1,0:T(8,128)} %bitcast.6, s32[64,128]{1,0:T(8,128)} %bitcast.7, bf16[6,256,256]{2,1,0:T(8,128)(2,1)} %constant.2.clone.tab_hbm), custom_call_target="tpu_custom_call" | custom-call | tf_op jit(solution)/shard_map/exchange/pallas_call | solution.py:444
  32.2 0.7 %copy.7 = f32[1,2,128,128]{3,2,1,0:T(8,128)} copy(f32[1,2,128,128]{3,2,1,0:T(8,128)S(1)} %bitcast.4) | data formatting | bytes 262144
  32.9 0.6 %copy.8 = f32[1,128,128]{2,1,0:T(8,128)} copy(f32[1,128,128]{2,1,0:T(8,128)S(1)} %bitcast.5) | data formatting | bytes 131072
